TPU v7x, 32 devices: a whole 2x2x4 slice. The times are simulated.
32 devices in a mesh: groups: 2 (over y), rows: 4 (over z), cols: 4 (over x, core).
Axes of the slice: x: 2, y: 2, z: 4, core: 2. Of those that a mesh axis runs over, the one named last changes fastest.
Arguments:
- coupling: bfloat16 [6, 8192, 8192], P('groups', 'cols', 'rows'), parts along dimension 0, may hold values from -0.0625 to 0.0625
- diag_inverse: bfloat16 [6, 8192, 8192], P('groups', 'rows', 'cols'), parts along dimension 0, as said below
- loads: bfloat16 [6, 128, 8192], P('groups', None, 'cols'), parts along dimension 0, may hold values from -6 to 6
- axle_index: int32 [64], P('groups'), parts along dimension 0, may hold values from 0 to 127
Outputs:
- influence: float32 [6, 32, 8192], P('groups', None, 'cols'), parts along dimension 0
- forward: float32 [6, 32, 8192], P('groups', None, 'rows'), parts along dimension 0
There are 2 independent parts, one for each index of `groups`. A program takes and returns all parts, laid end to end along the dimension named above; each array names one. Nothing has to cross between parts.
Inputs may be any that keep to these rules, and one draw needn't show every extreme that they name: `diag_inverse`: lower triangular with a positive diagonal.
All inputs are finite; a program needn't handle non-finite values.
Results may differ from a plain program's by a relative error of at most 0.0065.
Values sent between devices are 32-bit elements; how exact they have to be, the bound alone decides.
No kernel may reach another device: no remote copies, remote signals or barrier semaphores. Data moves between devices by JAX's collectives and lax.ppermute only.
A program may use at most 128 MiB of HBM per device.

v0:
```python
import jax
import jax.numpy as jnp
from jax import lax
from jax.sharding import PartitionSpec as P

LEVELS = 3


def pair_index(high, low):
    return high * (high - 1) // 2 + low


def forward_couple(partial_value):
    return lax.psum(partial_value, "rows")


def forward_diag(resid, tile):
    partial_value = jnp.einsum(
        "lm,im->li", resid.astype(jnp.bfloat16), tile, preferred_element_type=jnp.float32
    )
    return lax.psum(partial_value, "cols")


def backward_couple(partial_value):
    return lax.psum(partial_value, "cols")


def backward_diag(resid, tile):
    partial_value = jnp.einsum(
        "li,im->lm", resid.astype(jnp.bfloat16), tile, preferred_element_type=jnp.float32
    )
    return lax.psum(partial_value, "rows")


def lower_term(vector_bf, block):
    return jnp.einsum("lj,ij->li", vector_bf, block, preferred_element_type=jnp.float32)


def upper_term(vector_bf, block):
    return jnp.einsum("li,ij->lj", vector_bf, block, preferred_element_type=jnp.float32)


def solve_batch(rhs, coupling, diag_inverse):
    solved = []
    solved_bf = []
    for level in range(LEVELS):
        resid = rhs[level]
        if level > 0:
            partial_value = lower_term(solved_bf[0], coupling[pair_index(level, 0)])
            for lower in range(1, level):
                partial_value = partial_value + lower_term(
                    solved_bf[lower], coupling[pair_index(level, lower)]
                )
            resid = resid - forward_couple(partial_value)
        value = forward_diag(resid, diag_inverse[level])
        solved.append(value)
        solved_bf.append(value.astype(jnp.bfloat16))
    answers = [None] * LEVELS
    answers_bf = [None] * LEVELS
    for level in range(LEVELS - 1, -1, -1):
        resid = solved[level]
        if level < LEVELS - 1:
            partial_value = upper_term(
                answers_bf[LEVELS - 1], coupling[pair_index(LEVELS - 1, level)]
            )
            for upper in range(level + 1, LEVELS - 1):
                partial_value = partial_value + upper_term(
                    answers_bf[upper], coupling[pair_index(upper, level)]
                )
            resid = resid - backward_couple(partial_value)
        value = backward_diag(resid, diag_inverse[level])
        answers[level] = value
        answers_bf[level] = value.astype(jnp.bfloat16)
    return (jnp.stack(answers), jnp.stack(solved))


def body(coupling, diag_inverse, loads, axle_index):
    positions = loads.shape[1]
    selector = (axle_index[:, None] == jnp.arange(positions, dtype=jnp.int32)[None, :]).astype(
        jnp.bfloat16
    )
    rhs = jnp.einsum("lp,kpc->klc", selector, loads, preferred_element_type=jnp.float32)
    answer, solved = solve_batch(rhs, coupling, diag_inverse)
    return (answer, solved)


def solution(mesh):
    placed = (
        P("groups", "cols", "rows"),
        P("groups", "rows", "cols"),
        P("groups", None, "cols"),
        P("groups"),
    )
    return jax.shard_map(
        body,
        mesh=mesh,
        in_specs=placed,
        out_specs=(P("groups", None, "cols"), P("groups", None, "rows")),
        check_vma=False,
    )
```

profile of v0, /device:TPU:0, one launch (start us, length us, event | category | flops | bytes accessed | tf_op | source)
XLA Modules:
  0.0 431.7 jit_solution(7310455258160250758)
XLA Ops:
  7.2 0.0 copy-start
  7.2 0.0 all-reduce.11.cloned.1.call-start
  7.2 1.4 copy-done
  8.6 1.0 convolution_bitcast_fusion
  9.6 6.7 %fusion.22 = f32[32,2048]{1,0:T(8,128)} fusion(bf16[3,2048,2048]{2,1,0:T(8,128)(2,1)} %param.5, f32[3,32,2048]{2,1,0:T(8,128)S(1)} %convolution_bitcast_fusion), kind=kOutput, calls=%fused_computation.22 | convolution fusion | flops 268435456 | bytes 8781824 | tf_op jit(solution)/shard_map/lm,im->li/dot_general | solution.py:18
  16.3 0.0 all-reduce.11.cloned.1.call-update
  16.3 0.0 all-reduce.13.cloned.1.call-start
  16.4 34.8 %all-reduce.11.cloned.1.call-done = f32[32,2048]{1,0:T(8,128)} async-done(((f32[32,2048]{1,0:T(8,128)}), f32[32,2048]{1,0:T(8,128)}) %all-reduce.11.cloned.1.call-update) | async-done | bytes 262160 | tf_op jit(solution)/shard_map/psum | solution.py:21
  51.1 6.8 %fusion.14 = f32[32,2048]{1,0:T(8,128)} fusion(bf16[3,2048,2048]{2,1,0:T(8,128)(2,1)} %param.4, f32[32,2048]{1,0:T(8,128)} %all-reduce.11.cloned.1.call-done), kind=kOutput, calls=%fused_computation.14 | convolution fusion | flops 268500992 | bytes 8912896 | tf_op jit(solution)/shard_map/lj,ij->li/dot_general | solution.py:36
  57.9 0.0 all-reduce.13.cloned.1.call-update
  58.0 0.0 all-reduce.15.cloned.1.call-start
  58.0 35.4 %all-reduce.13.cloned.1.call-done = f32[32,2048]{1,0:T(8,128)} async-done(((f32[32,2048]{1,0:T(8,128)}), f32[32,2048]{1,0:T(8,128)}) %all-reduce.13.cloned.1.call-update) | async-done | bytes 262160 | tf_op jit(solution)/shard_map/psum | solution.py:14
  93.4 6.8 %fusion.10 = f32[32,2048]{1,0:T(8,128)} fusion(bf16[3,2048,2048]{2,1,0:T(8,128)(2,1)} %param.5, f32[32,2048]{1,0:T(8,128)} %all-reduce.13.cloned.1.call-done, f32[3,32,2048]{2,1,0:T(8,128)S(1)} %convolution_bitcast_fusion), kind=kOutput, calls=%fused_computation.10 | convolution fusion | flops 268566528 | bytes 9175040 | tf_op jit(solution)/shard_map/lm,im->li/dot_general | solution.py:18
  100.2 0.0 all-reduce.15.cloned.1.call-update
  100.2 0.0 all-reduce.17.cloned.1.call-start
  100.3 31.8 %all-reduce.15.cloned.1.call-done = f32[32,2048]{1,0:T(8,128)} async-done(((f32[32,2048]{1,0:T(8,128)}), f32[32,2048]{1,0:T(8,128)}) %all-reduce.15.cloned.1.call-update) | async-done | bytes 262160 | tf_op jit(solution)/shard_map/psum | solution.py:21
  132.1 6.1 %fusion.6 = f32[32,2048]{1,0:T(8,128)S(1)} fusion(bf16[3,2048,2048]{2,1,0:T(8,128)(2,1)} %param.4, f32[32,2048]{1,0:T(8,128)} %all-reduce.15.cloned.1.call-done), kind=kOutput, calls=%fused_computation.6 | convolution fusion | flops 268500992 | bytes 8912896 | tf_op jit(solution)/shard_map/lj,ij->li/dot_general | solution.py:36
  138.2 0.0 copy-done.1
  138.2 6.7 %fusion.39 = f32[32,2048]{1,0:T(8,128)} fusion(f32[32,2048]{1,0:T(8,128)S(1)} %fusion.6, bf16[3,2048,2048]{2,1,0:T(8,128)(2,1)} %param.4, f32[32,2048]{1,0:T(8,128)S(1)} %copy-done.1), kind=kOutput, calls=%fused_computation.38 | convolution fusion | flops 268566528 | bytes 9175040 | tf_op jit(solution)/shard_map/lj,ij->li/dot_general | solution.py:36
  144.9 0.0 all-reduce.17.cloned.1.call-update
  144.9 0.2 all-reduce.19.cloned.1.call-start
  145.1 35.3 %all-reduce.17.cloned.1.call-done = f32[32,2048]{1,0:T(8,128)} async-done(((f32[32,2048]{1,0:T(8,128)}), f32[32,2048]{1,0:T(8,128)}) %all-reduce.17.cloned.1.call-update) | async-done | bytes 262160 | tf_op jit(solution)/shard_map/psum | solution.py:14
  180.4 6.8 %fusion.2 = f32[32,2048]{1,0:T(8,128)} fusion(bf16[3,2048,2048]{2,1,0:T(8,128)(2,1)} %param.5, f32[32,2048]{1,0:T(8,128)} %all-reduce.17.cloned.1.call-done, f32[3,32,2048]{2,1,0:T(8,128)S(1)} %convolution_bitcast_fusion), kind=kOutput, calls=%fused_computation.2 | convolution fusion | flops 268566528 | bytes 9175040 | tf_op jit(solution)/shard_map/lm,im->li/dot_general | solution.py:18
  187.2 0.0 all-reduce.19.cloned.1.call-update
  187.2 0.0 all-reduce.21.cloned.1.call-start
  187.2 31.8 %all-reduce.19.cloned.1.call-done = f32[32,2048]{1,0:T(8,128)} async-done(((f32[32,2048]{1,0:T(8,128)}), f32[32,2048]{1,0:T(8,128)}) %all-reduce.19.cloned.1.call-update) | async-done | bytes 262160 | tf_op jit(solution)/shard_map/psum | solution.py:21
  219.0 5.7 %fusion = f32[32,2048]{1,0:T(8,128)} fusion(bf16[3,2048,2048]{2,1,0:T(8,128)(2,1)} %param.5, f32[32,2048]{1,0:T(8,128)} %all-reduce.19.cloned.1.call-done), kind=kOutput, calls=%fused_computation | convolution fusion | flops 268500992 | bytes 8912896 | tf_op jit(solution)/shard_map/li,im->lm/dot_general | solution.py:29
  224.8 0.0 all-reduce.21.cloned.1.call-update
  224.8 0.0 all-reduce.23.cloned.1.call-start
  224.8 35.4 %all-reduce.21.cloned.1.call-done = f32[32,2048]{1,0:T(8,128)} async-done(((f32[32,2048]{1,0:T(8,128)}), f32[32,2048]{1,0:T(8,128)}) %all-reduce.21.cloned.1.call-update) | async-done | bytes 262160 | tf_op jit(solution)/shard_map/psum | solution.py:32
  260.3 5.7 %fusion.4 = f32[32,2048]{1,0:T(8,128)} fusion(bf16[3,2048,2048]{2,1,0:T(8,128)(2,1)} %param.4, f32[32,2048]{1,0:T(8,128)} %all-reduce.21.cloned.1.call-done), kind=kOutput, calls=%fused_computation.4 | convolution fusion | flops 268500992 | bytes 8912896 | tf_op jit(solution)/shard_map/li,ij->lj/dot_general | solution.py:40
  266.0 0.0 all-reduce.23.cloned.1.call-update
  266.0 0.0 all-reduce.25.cloned.1.call-start
  266.1 31.8 %all-reduce.23.cloned.1.call-done = f32[32,2048]{1,0:T(8,128)} async-done(((f32[32,2048]{1,0:T(8,128)}), f32[32,2048]{1,0:T(8,128)}) %all-reduce.23.cloned.1.call-update) | async-done | bytes 262160 | tf_op jit(solution)/shard_map/psum | solution.py:25
  297.9 5.7 %fusion.8 = f32[32,2048]{1,0:T(8,128)} fusion(bf16[3,2048,2048]{2,1,0:T(8,128)(2,1)} %param.5, f32[32,2048]{1,0:T(8,128)S(1)} %copy-done.2, f32[32,2048]{1,0:T(8,128)} %all-reduce.23.cloned.1.call-done), kind=kOutput, calls=%fused_computation.8 | convolution fusion | flops 268566528 | bytes 9175040 | tf_op jit(solution)/shard_map/li,im->lm/dot_general | solution.py:29
  303.6 0.0 all-reduce.25.cloned.1.call-update
  303.6 0.0 all-reduce.27.cloned.1.call-start
  303.7 35.4 %all-reduce.25.cloned.1.call-done = f32[32,2048]{1,0:T(8,128)} async-done(((f32[32,2048]{1,0:T(8,128)}), f32[32,2048]{1,0:T(8,128)}) %all-reduce.25.cloned.1.call-update) | async-done | bytes 262160 | tf_op jit(solution)/shard_map/psum | solution.py:32
  339.1 5.0 %fusion.12 = f32[32,2048]{1,0:T(8,128)S(1)} fusion(bf16[3,2048,2048]{2,1,0:T(8,128)(2,1)} %param.4, f32[32,2048]{1,0:T(8,128)} %all-reduce.25.cloned.1.call-done), kind=kOutput, calls=%fused_computation.12 | convolution fusion | flops 268500992 | bytes 8912896 | tf_op jit(solution)/shard_map/li,ij->lj/dot_general | solution.py:40
  344.2 5.7 %fusion.42 = f32[32,2048]{1,0:T(8,128)} fusion(f32[32,2048]{1,0:T(8,128)S(1)} %fusion.12, bf16[3,2048,2048]{2,1,0:T(8,128)(2,1)} %param.4, f32[32,2048]{1,0:T(8,128)S(1)} %copy-done.3), kind=kOutput, calls=%fused_computation.39 | convolution fusion | flops 268566528 | bytes 9175040 | tf_op jit(solution)/shard_map/li,ij->lj/dot_general | solution.py:40
  349.9 0.0 all-reduce.27.cloned.1.call-update
  349.9 0.0 all-reduce.29.cloned.1.call-start
  349.9 31.8 %all-reduce.27.cloned.1.call-done = f32[32,2048]{1,0:T(8,128)} async-done(((f32[32,2048]{1,0:T(8,128)}), f32[32,2048]{1,0:T(8,128)}) %all-reduce.27.cloned.1.call-update) | async-done | bytes 262160 | tf_op jit(solution)/shard_map/psum | solution.py:25
  381.7 5.7 %fusion.36 = f32[1,32,2048]{2,1,0:T(8,128)} fusion(bf16[3,2048,2048]{2,1,0:T(8,128)(2,1)} %param.5, f32[32,2048]{1,0:T(8,128)S(1)} %copy-done.1, f32[32,2048]{1,0:T(8,128)} %all-reduce.27.cloned.1.call-done), kind=kOutput, calls=%fused_computation.37 | convolution fusion | flops 268566528 | bytes 9175040 | tf_op jit(solution)/shard_map/li,im->lm/dot_general | solution.py:29
  387.5 0.0 all-reduce.29.cloned.1.call-update
  387.5 0.9 pad_maximum_fusion.1
  388.4 34.5 %all-reduce.29.cloned.1.call-done = f32[1,32,2048]{2,1,0:T(8,128)} async-done(((f32[1,32,2048]{2,1,0:T(8,128)}), f32[1,32,2048]{2,1,0:T(8,128)}) %all-reduce.29.cloned.1.call-update) | async-done | bytes 262160 | tf_op jit(solution)/shard_map/psum | solution.py:32
  423.0 1.9 pad_maximum_fusion
  (9 shorter events, 0.0 us)
Async XLA Ops:
  7.2 1.4 copy-start
  7.2 44.0 %all-reduce.11.cloned.1.call-start = ((), (), s32[]{:S(2)}) async-start(), calls=%async_computation | async-start | bytes 524288 | tf_op jit(solution)/shard_map/psum | solution.py:21
  16.3 77.1 %all-reduce.13.cloned.1.call-start = ((), (), s32[]{:S(2)}) async-start(), calls=%async_computation.1 | async-start | bytes 524288 | tf_op jit(solution)/shard_map/psum | solution.py:14
  57.9 80.2 %copy-start.1 = (f32[32,2048]{1,0:T(8,128)S(1)}, f32[32,2048]{1,0:T(8,128)}, u32[]{:S(2)}) copy-start(f32[32,2048]{1,0:T(8,128)} %all-reduce.11.cloned.1.call-done) | copy-start | bytes 786436
  58.0 74.1 %all-reduce.15.cloned.1.call-start = ((), (), s32[]{:S(2)}) async-start(), calls=%async_computation.2 | async-start | bytes 524288 | tf_op jit(solution)/shard_map/psum | solution.py:21
  100.2 80.1 %all-reduce.17.cloned.1.call-start = ((), (), s32[]{:S(2)}) async-start(), calls=%async_computation.3 | async-start | bytes 524288 | tf_op jit(solution)/shard_map/psum | solution.py:14
  144.9 74.1 %all-reduce.19.cloned.1.call-start = ((), (), s32[]{:S(2)}) async-start(), calls=%async_computation.4 | async-start | bytes 524288 | tf_op jit(solution)/shard_map/psum | solution.py:21
  187.2 110.7 %copy-start.2 = (f32[32,2048]{1,0:T(8,128)S(1)}, f32[32,2048]{1,0:T(8,128)}, u32[]{:S(2)}) copy-start(f32[32,2048]{1,0:T(8,128)} %all-reduce.15.cloned.1.call-done) | copy-start | bytes 786436
  187.2 73.1 %all-reduce.21.cloned.1.call-start = ((), (), s32[]{:S(2)}) async-start(), calls=%async_computation.5 | async-start | bytes 524288 | tf_op jit(solution)/shard_map/psum | solution.py:32
  224.8 73.1 %all-reduce.23.cloned.1.call-start = ((), (), s32[]{:S(2)}) async-start(), calls=%async_computation.6 | async-start | bytes 524288 | tf_op jit(solution)/shard_map/psum | solution.py:25
  266.0 78.1 %copy-start.3 = (f32[32,2048]{1,0:T(8,128)S(1)}, f32[32,2048]{1,0:T(8,128)}, u32[]{:S(2)}) copy-start(f32[32,2048]{1,0:T(8,128)} %all-reduce.21.cloned.1.call-done) | copy-start | bytes 786436
  266.0 73.1 %all-reduce.25.cloned.1.call-start = ((), (), s32[]{:S(2)}) async-start(), calls=%async_computation.7 | async-start | bytes 524288 | tf_op jit(solution)/shard_map/psum | solution.py:32
  303.6 78.1 %all-reduce.27.cloned.1.call-start = ((), (), s32[]{:S(2)}) async-start(), calls=%async_computation.8 | async-start | bytes 524288 | tf_op jit(solution)/shard_map/psum | solution.py:25
  344.2 43.3 %copy-start.4 = (f32[32,2048]{1,0:T(8,128)S(1)}, f32[32,2048]{1,0:T(8,128)}, u32[]{:S(2)}) copy-start(f32[32,2048]{1,0:T(8,128)} %all-reduce.19.cloned.1.call-done) | copy-start | bytes 786436
  344.2 78.8 %copy-start.5 = (f32[32,2048]{1,0:T(8,128)S(1)}, f32[32,2048]{1,0:T(8,128)}, u32[]{:S(2)}) copy-start(f32[32,2048]{1,0:T(8,128)} %all-reduce.25.cloned.1.call-done) | copy-start | bytes 786436
  349.9 73.1 %all-reduce.29.cloned.1.call-start = ((), (), s32[]{:S(2)}) async-start(), calls=%async_computation.9 | async-start | bytes 524288 | tf_op jit(solution)/shard_map/psum | solution.py:32
Sparse Core Ops, SparseCore 0:
  16.4 34.6 all-reduce.10
  58.1 35.3 all-reduce.12
  100.4 31.6 all-reduce.14
  145.0 35.3 all-reduce.16
  187.3 31.6 all-reduce.18
  224.9 35.3 all-reduce.20
  266.1 31.6 all-reduce.22
  303.8 35.3 all-reduce.24
  350.0 31.6 all-reduce.26
  387.6 35.2 all-reduce.28
where the time goes:
time: 432 us
  waiting for transfers between devices  338 us (78%)
  matrix products  74.4 us (17%)
  between operations  14.2 us (3%)
    psum x3, waiting for transfers between devices, backward_diag(): return lax.psum(partial_value, 'rows')  105 us
    psum x3, waiting for transfers between devices, forward_diag(): return lax.psum(partial_value, 'cols')  98.4 us
    psum x2, waiting for transfers between devices, forward_couple(): return lax.psum(partial_value, 'rows')  70.7 us
    psum x2, waiting for transfers between devices, backward_couple(): return lax.psum(partial_value, 'cols')  63.6 us
    dot_general x3, matrix products, forward_diag(): jnp.einsum('lm,im->li', resid.astype(jnp.bfloat16), tile, preferred_eleme...  20.2 us
    dot_general x3, matrix products, lower_term(): jnp.einsum('lj,ij->li', vector_bf, block, preferred_element_type=jnp.floa...  19.5 us
    dot_general x3, matrix products, backward_diag(): jnp.einsum('li,im->lm', resid.astype(jnp.bfloat16), tile, preferred_eleme...  17.2 us
    dot_general x3, matrix products, upper_term(): jnp.einsum('li,ij->lj', vector_bf, block, preferred_element_type=jnp.floa...  16.4 us
  transfers between devices with their start and end apart: 10, of which 10 were waited for; matrix products, arithmetic and copies ran while one was open for 0% of the time, Pallas kernels for 0%

commit v1 on v0

--- a/solution.py
+++ b/solution.py
@@ -18,7 +18,7 @@
     partial_value = jnp.einsum(
         "lm,im->li", resid.astype(jnp.bfloat16), tile, preferred_element_type=jnp.float32
     )
-    return lax.psum(partial_value, "cols")
+    return jnp.sum(lax.all_gather(partial_value, "cols"), 0)
 
 
 def backward_couple(partial_value):

time: 432 us -> 390 us (0.903)
  waiting for transfers between devices: 338 us -> 292 us
    psum x3 -> x0, waiting for transfers between devices: 98.4 us -> none  [forward_diag(): return lax.psum(partial_value, 'cols')]
    all_gather x0 -> x3, waiting for transfers between devices: none -> 52.6 us  [forward_diag(): return jnp.sum(lax.all_gather(partial_value, 'cols'), 0)]
where the time goes in v1:
time: 390 us
  waiting for transfers between devices  292 us (75%)
  matrix products  74.1 us (19%)
  between operations  14.2 us (4%)
  other arithmetic  6.73 us (2%)
    psum x3, waiting for transfers between devices, backward_diag(): return lax.psum(partial_value, 'rows')  105 us
    psum x2, waiting for transfers between devices, forward_couple(): return lax.psum(partial_value, 'rows')  70.7 us
    psum x2, waiting for transfers between devices, backward_couple(): return lax.psum(partial_value, 'cols')  63.6 us
    all_gather x3, waiting for transfers between devices, forward_diag(): return jnp.sum(lax.all_gather(partial_value, 'cols'), 0)  52.6 us
    dot_general x3, matrix products, forward_diag(): jnp.einsum('lm,im->li', resid.astype(jnp.bfloat16), tile, preferred_eleme...  20.2 us
    dot_general x3, matrix products, lower_term(): jnp.einsum('lj,ij->li', vector_bf, block, preferred_element_type=jnp.floa...  19.3 us
    dot_general x3, matrix products, backward_diag(): jnp.einsum('li,im->lm', resid.astype(jnp.bfloat16), tile, preferred_eleme...  17.1 us
    dot_general x3, matrix products, upper_term(): jnp.einsum('li,ij->lj', vector_bf, block, preferred_element_type=jnp.floa...  16.4 us
  transfers between devices with their start and end apart: 10, of which 10 were waited for; matrix products, arithmetic and copies ran while one was open for 0% of the time, Pallas kernels for 0%

profile of v1, /device:TPU:0, one launch (start us, length us, event | category | flops | bytes accessed | tf_op | source)
XLA Modules:
  0.0 389.6 jit_solution(5442025086355451501)
XLA Ops:
  7.2 0.0 all-gather.7.cloned.1.call-start
  7.2 1.4 copy-done
  8.6 1.0 convolution_bitcast_fusion
  9.6 6.7 %fusion.22 = f32[32,2048]{1,0:T(8,128)} fusion(bf16[3,2048,2048]{2,1,0:T(8,128)(2,1)} %param.5, f32[3,32,2048]{2,1,0:T(8,128)S(1)} %convolution_bitcast_fusion), kind=kOutput, calls=%fused_computation.22 | convolution fusion | flops 268435456 | bytes 8781824 | tf_op jit(solution)/shard_map/lm,im->li/dot_general | solution.py:18
  16.3 0.0 all-gather.7.cloned.1.call-update
  16.3 0.0 all-reduce.8.cloned.1.call-start
  16.4 19.5 %all-gather.7.cloned.1.call-done = f32[128,2048]{1,0:T(8,128)} async-done(((f32[32,2048]{1,0:T(8,128)}), f32[128,2048]{1,0:T(8,128)}) %all-gather.7.cloned.1.call-update) | async-done | bytes 1048592 | tf_op jit(solution)/shard_map/all_gather | solution.py:21
  35.9 1.3 reduce_sum.27
  37.2 6.7 %fusion.14 = f32[32,2048]{1,0:T(8,128)} fusion(bf16[3,2048,2048]{2,1,0:T(8,128)(2,1)} %param.4, f32[32,2048]{1,0:T(8,128)S(1)} %reduce_sum.27), kind=kOutput, calls=%fused_computation.14 | convolution fusion | flops 268500992 | bytes 8912896 | tf_op jit(solution)/shard_map/lj,ij->li/dot_general | solution.py:36
  43.9 0.0 all-reduce.8.cloned.1.call-update
  43.9 0.0 all-gather.9.cloned.1.call-start
  44.0 35.5 %all-reduce.8.cloned.1.call-done = f32[32,2048]{1,0:T(8,128)} async-done(((f32[32,2048]{1,0:T(8,128)}), f32[32,2048]{1,0:T(8,128)}) %all-reduce.8.cloned.1.call-update) | async-done | bytes 262160 | tf_op jit(solution)/shard_map/psum | solution.py:14
  79.4 6.8 %fusion.10 = f32[32,2048]{1,0:T(8,128)} fusion(bf16[3,2048,2048]{2,1,0:T(8,128)(2,1)} %param.5, f32[32,2048]{1,0:T(8,128)} %all-reduce.8.cloned.1.call-done, f32[3,32,2048]{2,1,0:T(8,128)S(1)} %convolution_bitcast_fusion), kind=kOutput, calls=%fused_computation.10 | convolution fusion | flops 268566528 | bytes 9175040 | tf_op jit(solution)/shard_map/lm,im->li/dot_general | solution.py:18
  86.2 0.0 all-gather.9.cloned.1.call-update
  86.2 0.0 all-reduce.10.cloned.1.call-start
  86.3 16.6 %all-gather.9.cloned.1.call-done = f32[128,2048]{1,0:T(8,128)} async-done(((f32[32,2048]{1,0:T(8,128)}), f32[128,2048]{1,0:T(8,128)}) %all-gather.9.cloned.1.call-update) | async-done | bytes 1048592 | tf_op jit(solution)/shard_map/all_gather | solution.py:21
  102.8 1.3 reduce_sum.28
  104.1 6.0 %fusion.6 = f32[32,2048]{1,0:T(8,128)S(1)} fusion(bf16[3,2048,2048]{2,1,0:T(8,128)(2,1)} %param.4, f32[32,2048]{1,0:T(8,128)S(1)} %reduce_sum.28), kind=kOutput, calls=%fused_computation.6 | convolution fusion | flops 268500992 | bytes 8912896 | tf_op jit(solution)/shard_map/lj,ij->li/dot_general | solution.py:36
  110.1 6.7 %fusion.39 = f32[32,2048]{1,0:T(8,128)} fusion(f32[32,2048]{1,0:T(8,128)S(1)} %fusion.6, bf16[3,2048,2048]{2,1,0:T(8,128)(2,1)} %param.4, f32[32,2048]{1,0:T(8,128)S(1)} %reduce_sum.27), kind=kOutput, calls=%fused_computation.38 | convolution fusion | flops 268566528 | bytes 9175040 | tf_op jit(solution)/shard_map/lj,ij->li/dot_general | solution.py:36
  116.8 0.0 all-reduce.10.cloned.1.call-update
  116.8 0.2 all-gather.11.cloned.1.call-start
  117.1 35.2 %all-reduce.10.cloned.1.call-done = f32[32,2048]{1,0:T(8,128)} async-done(((f32[32,2048]{1,0:T(8,128)}), f32[32,2048]{1,0:T(8,128)}) %all-reduce.10.cloned.1.call-update) | async-done | bytes 262160 | tf_op jit(solution)/shard_map/psum | solution.py:14
  152.3 6.8 %fusion.2 = f32[32,2048]{1,0:T(8,128)} fusion(bf16[3,2048,2048]{2,1,0:T(8,128)(2,1)} %param.5, f32[32,2048]{1,0:T(8,128)} %all-reduce.10.cloned.1.call-done, f32[3,32,2048]{2,1,0:T(8,128)S(1)} %convolution_bitcast_fusion), kind=kOutput, calls=%fused_computation.2 | convolution fusion | flops 268566528 | bytes 9175040 | tf_op jit(solution)/shard_map/lm,im->li/dot_general | solution.py:18
  159.1 0.0 all-reduce.12.cloned.1.call-start
  159.1 16.6 %all-gather.11.cloned.1.call-done = f32[128,2048]{1,0:T(8,128)} async-done(((f32[32,2048]{1,0:T(8,128)}), f32[128,2048]{1,0:T(8,128)}) %all-gather.11.cloned.1.call-update) | async-done | bytes 1048592 | tf_op jit(solution)/shard_map/all_gather | solution.py:21
  175.7 1.3 reduce_sum.29
  177.0 5.6 %fusion = f32[32,2048]{1,0:T(8,128)} fusion(bf16[3,2048,2048]{2,1,0:T(8,128)(2,1)} %param.5, f32[32,2048]{1,0:T(8,128)S(1)} %reduce_sum.29), kind=kOutput, calls=%fused_computation | convolution fusion | flops 268500992 | bytes 8912896 | tf_op jit(solution)/shard_map/li,im->lm/dot_general | solution.py:29
  182.6 0.0 all-reduce.12.cloned.1.call-update
  182.7 0.0 all-reduce.14.cloned.1.call-start
  182.7 35.5 %all-reduce.12.cloned.1.call-done = f32[32,2048]{1,0:T(8,128)} async-done(((f32[32,2048]{1,0:T(8,128)}), f32[32,2048]{1,0:T(8,128)}) %all-reduce.12.cloned.1.call-update) | async-done | bytes 262160 | tf_op jit(solution)/shard_map/psum | solution.py:32
  218.2 5.7 %fusion.4 = f32[32,2048]{1,0:T(8,128)} fusion(bf16[3,2048,2048]{2,1,0:T(8,128)(2,1)} %param.4, f32[32,2048]{1,0:T(8,128)} %all-reduce.12.cloned.1.call-done), kind=kOutput, calls=%fused_computation.4 | convolution fusion | flops 268500992 | bytes 8912896 | tf_op jit(solution)/shard_map/li,ij->lj/dot_general | solution.py:40
  223.9 0.0 all-reduce.14.cloned.1.call-update
  223.9 0.0 all-reduce.16.cloned.1.call-start
  224.0 31.8 %all-reduce.14.cloned.1.call-done = f32[32,2048]{1,0:T(8,128)} async-done(((f32[32,2048]{1,0:T(8,128)}), f32[32,2048]{1,0:T(8,128)}) %all-reduce.14.cloned.1.call-update) | async-done | bytes 262160 | tf_op jit(solution)/shard_map/psum | solution.py:25
  255.8 5.7 %fusion.8 = f32[32,2048]{1,0:T(8,128)} fusion(bf16[3,2048,2048]{2,1,0:T(8,128)(2,1)} %param.5, f32[32,2048]{1,0:T(8,128)S(1)} %reduce_sum.28, f32[32,2048]{1,0:T(8,128)} %all-reduce.14.cloned.1.call-done), kind=kOutput, calls=%fused_computation.8 | convolution fusion | flops 268566528 | bytes 9175040 | tf_op jit(solution)/shard_map/li,im->lm/dot_general | solution.py:29
  261.5 0.0 all-reduce.16.cloned.1.call-update
  261.5 0.0 all-reduce.18.cloned.1.call-start
  261.6 35.4 %all-reduce.16.cloned.1.call-done = f32[32,2048]{1,0:T(8,128)} async-done(((f32[32,2048]{1,0:T(8,128)}), f32[32,2048]{1,0:T(8,128)}) %all-reduce.16.cloned.1.call-update) | async-done | bytes 262160 | tf_op jit(solution)/shard_map/psum | solution.py:32
  297.0 5.0 %fusion.12 = f32[32,2048]{1,0:T(8,128)S(1)} fusion(bf16[3,2048,2048]{2,1,0:T(8,128)(2,1)} %param.4, f32[32,2048]{1,0:T(8,128)} %all-reduce.16.cloned.1.call-done), kind=kOutput, calls=%fused_computation.12 | convolution fusion | flops 268500992 | bytes 8912896 | tf_op jit(solution)/shard_map/li,ij->lj/dot_general | solution.py:40
  302.0 5.7 %fusion.42 = f32[32,2048]{1,0:T(8,128)} fusion(f32[32,2048]{1,0:T(8,128)S(1)} %fusion.12, bf16[3,2048,2048]{2,1,0:T(8,128)(2,1)} %param.4, f32[32,2048]{1,0:T(8,128)S(1)} %copy-done.1), kind=kOutput, calls=%fused_computation.39 | convolution fusion | flops 268566528 | bytes 9175040 | tf_op jit(solution)/shard_map/li,ij->lj/dot_general | solution.py:40
  307.7 0.0 all-reduce.18.cloned.1.call-update
  307.8 0.0 all-reduce.20.cloned.1.call-start
  307.8 31.8 %all-reduce.18.cloned.1.call-done = f32[32,2048]{1,0:T(8,128)} async-done(((f32[32,2048]{1,0:T(8,128)}), f32[32,2048]{1,0:T(8,128)}) %all-reduce.18.cloned.1.call-update) | async-done | bytes 262160 | tf_op jit(solution)/shard_map/psum | solution.py:25
  339.6 5.7 %fusion.36 = f32[1,32,2048]{2,1,0:T(8,128)} fusion(bf16[3,2048,2048]{2,1,0:T(8,128)(2,1)} %param.5, f32[32,2048]{1,0:T(8,128)S(1)} %reduce_sum.27, f32[32,2048]{1,0:T(8,128)} %all-reduce.18.cloned.1.call-done), kind=kOutput, calls=%fused_computation.37 | convolution fusion | flops 268566528 | bytes 9175040 | tf_op jit(solution)/shard_map/li,im->lm/dot_general | solution.py:29
  345.3 0.0 all-reduce.20.cloned.1.call-update
  345.4 0.9 pad_maximum_fusion.1
  346.3 34.5 %all-reduce.20.cloned.1.call-done = f32[1,32,2048]{2,1,0:T(8,128)} async-done(((f32[1,32,2048]{2,1,0:T(8,128)}), f32[1,32,2048]{2,1,0:T(8,128)}) %all-reduce.20.cloned.1.call-update) | async-done | bytes 262160 | tf_op jit(solution)/shard_map/psum | solution.py:32
  380.8 1.9 pad_maximum_fusion
  (6 shorter events, 0.0 us)
Async XLA Ops:
  7.2 1.4 copy-start
  7.2 28.7 %all-gather.7.cloned.1.call-start = ((), (), s32[]{:S(2)}) async-start(), calls=%async_computation.7 | async-start | bytes 1310720 | tf_op jit(solution)/shard_map/all_gather | solution.py:21
  16.3 63.1 %all-reduce.8.cloned.1.call-start = ((), (), s32[]{:S(2)}) async-start(), calls=%async_computation | async-start | bytes 524288 | tf_op jit(solution)/shard_map/psum | solution.py:14
  43.9 58.9 %all-gather.9.cloned.1.call-start = ((), (), s32[]{:S(2)}) async-start(), calls=%async_computation.8 | async-start | bytes 1310720 | tf_op jit(solution)/shard_map/all_gather | solution.py:21
  86.2 66.1 %all-reduce.10.cloned.1.call-start = ((), (), s32[]{:S(2)}) async-start(), calls=%async_computation.1 | async-start | bytes 524288 | tf_op jit(solution)/shard_map/psum | solution.py:14
  116.8 58.9 %all-gather.11.cloned.1.call-start = ((), (), s32[]{:S(2)}) async-start(), calls=%async_computation.9 | async-start | bytes 1310720 | tf_op jit(solution)/shard_map/all_gather | solution.py:21
  159.1 59.1 %all-reduce.12.cloned.1.call-start = ((), (), s32[]{:S(2)}) async-start(), calls=%async_computation.2 | async-start | bytes 524288 | tf_op jit(solution)/shard_map/psum | solution.py:32
  182.7 73.1 %all-reduce.14.cloned.1.call-start = ((), (), s32[]{:S(2)}) async-start(), calls=%async_computation.3 | async-start | bytes 524288 | tf_op jit(solution)/shard_map/psum | solution.py:25
  223.9 78.1 %copy-start.1 = (f32[32,2048]{1,0:T(8,128)S(1)}, f32[32,2048]{1,0:T(8,128)}, u32[]{:S(2)}) copy-start(f32[32,2048]{1,0:T(8,128)} %all-reduce.12.cloned.1.call-done) | copy-start | bytes 786436
  223.9 73.1 %all-reduce.16.cloned.1.call-start = ((), (), s32[]{:S(2)}) async-start(), calls=%async_computation.4 | async-start | bytes 524288 | tf_op jit(solution)/shard_map/psum | solution.py:32
  261.5 78.1 %all-reduce.18.cloned.1.call-start = ((), (), s32[]{:S(2)}) async-start(), calls=%async_computation.5 | async-start | bytes 524288 | tf_op jit(solution)/shard_map/psum | solution.py:25
  302.0 78.8 %copy-start.2 = (f32[32,2048]{1,0:T(8,128)S(1)}, f32[32,2048]{1,0:T(8,128)}, u32[]{:S(2)}) copy-start(f32[32,2048]{1,0:T(8,128)} %all-reduce.16.cloned.1.call-done) | copy-start | bytes 786436
  307.8 73.1 %all-reduce.20.cloned.1.call-start = ((), (), s32[]{:S(2)}) async-start(), calls=%async_computation.6 | async-start | bytes 524288 | tf_op jit(solution)/shard_map/psum | solution.py:32
Sparse Core Ops, SparseCore 0:
  16.4 19.4 all-gather.6
  44.0 35.3 all-reduce.7
  86.3 16.4 all-gather.8
  117.0 35.2 all-reduce.9
  159.2 16.4 all-gather.10
  182.8 35.3 all-reduce.11
  224.1 31.6 all-reduce.13
  261.7 35.3 all-reduce.15
  307.9 31.6 all-reduce.17
  345.5 35.3 all-reduce.19
